TPU v7x, 256 devices: a whole 4x4x8 slice. The times are simulated.
256 devices in a mesh: ma: 64 (over x, z, core), lev: 4 (over y).
Axes of the slice: x: 4, y: 4, z: 8, core: 2. Of those that a mesh axis runs over, the one named last changes fastest.
Arguments:
- forcing: float32 [72, 2, 1280, 1280], P('lev', None, 'ma'), may hold values from -80 to 80
- coupling: float32 [4, 1280, 1280], P(None, 'ma'), may hold values from -0.3 to 0.3
- helmholtz: float32 [1280], replicated, may hold values from 0.5 to 5
- vertical: float32 [72, 72], replicated, may hold values from -1 to 3, as said below
Outputs:
- solution: float32 [72, 2, 1280, 1280], P('lev', None, 'ma')
- norms: float32 [2], replicated
Inputs may be any that keep to these rules, and one draw needn't show every extreme that they name: `vertical`: the diagonal entries lie between 1 and 3.
All inputs are finite; a program needn't handle non-finite values.
Results may differ from a plain program's by a relative error of at most 0.000071.
Values sent between devices are 32-bit elements; how exact they have to be, the bound alone decides.
No kernel may reach another device: no remote copies, remote signals or barrier semaphores. Data moves between devices by JAX's collectives and lax.ppermute only.
A program may use at most 192 MiB of HBM per device.

v0:
```python
import jax
import jax.numpy as jnp
from jax import lax
from jax.sharding import Mesh
from jax.sharding import PartitionSpec as P

LEV = 72
WAVES = 1280
MA = ("ma_0", "ma_1", "ma_2")
MA_LEV = ("ma_0", "ma_1", "ma_2", "lev")
OFFSETS = (-2, -1, 1, 2)


def shifted(block, axis, distance):
    devices = range(lax.axis_size(axis))
    route = [(i - distance, i) for i in devices if i - distance in devices]
    return lax.ppermute(block, axis, route)


def by_axis(x, axes):
    for axis in axes:
        x = lax.psum(x, axis)
    return x


def owned_waves(rows, owners, index):
    fold = jnp.arange(rows, dtype=jnp.int32)
    return fold * owners + jnp.where(fold % 2 == 0, index, owners - 1 - index)


def next_row(block, direction):
    empty = jnp.zeros_like(block[:, :, :1])
    if direction > 0:
        return jnp.concatenate([block[:, :, 1:], empty], axis=2)
    return jnp.concatenate([empty, block[:, :, :-1]], axis=2)


def coupled(nearby, offset, owners, index, rows):
    fold = jnp.arange(rows, dtype=jnp.int32)
    even_fold = fold % 2 == 0
    source = jnp.where(even_fold, index + offset, index - offset)
    inside = (source >= 0) & (source < owners)
    upper = 2 * owners - 1 - 2 * index
    lower = -1 - 2 * index
    beyond = jnp.where(
        even_fold,
        jnp.where(source >= owners, upper - offset, lower - offset),
        jnp.where(source < 0, lower + offset, upper + offset),
    )
    picked = jnp.where(even_fold[None, None, :, None], nearby[offset], nearby[-offset])
    result = picked * inside.astype(jnp.float32)[None, None, :, None]
    direction = 1 if offset > 0 else -1
    for delta in (-1, 0, 1):
        weight = (~inside & (beyond == delta)).astype(jnp.float32)
        result = result + next_row(nearby[delta], direction) * weight[None, None, :, None]
    return result


def square_neighbours(values):
    nearby = {0: values}
    for distance in (1, 2, -1, -2):
        nearby[-distance] = shifted(values, MA, distance)
    return nearby


def norm_total(value):
    return by_axis(value, MA_LEV)


def body(forcing, coupling, helmholtz, vertical):
    owners = lax.axis_size(MA)
    index = lax.axis_index(MA)
    rows = forcing.shape[2]
    waves = owned_waves(rows, owners, index)
    width = forcing.shape[3]
    levels = forcing.shape[0]
    weights = lax.dynamic_slice_in_dim(vertical, lax.axis_index("lev") * levels, levels, 0)
    diagonal = lax.dynamic_slice_in_dim(
        jnp.diagonal(vertical), lax.axis_index("lev") * levels, levels, 0
    )
    positions = jnp.arange(width, dtype=jnp.int32)
    live = (positions[None, :] >= waves[:, None]).astype(jnp.float32)[None, None]
    scale = (1.0 / (1.0 + helmholtz[None, :] * diagonal[:, None]))[:, None, None, :]
    rhs = forcing * live
    first_sum = norm_total(jnp.sum(rhs * rhs))
    first = scale * rhs
    mixed = jnp.einsum(
        "kl,lcin->kcin",
        weights,
        lax.all_gather(first, "lev", axis=0, tiled=True),
        precision=lax.Precision.HIGHEST,
    )
    nearby = square_neighbours(first)
    result = first + helmholtz[None, None, None, :] * mixed
    for place, offset in enumerate(OFFSETS):
        result = result + coupling[place][None, None] * coupled(nearby, offset, owners, index, rows)
    residual = rhs - result * live
    solution = first + scale * residual
    second_sum = norm_total(jnp.sum(residual * residual))
    count = LEV * WAVES * (WAVES + 1)
    norms = jnp.sqrt(jnp.stack([first_sum, second_sum]) / count)
    return (solution, norms)


def solution(mesh):
    split = Mesh(mesh.devices.reshape(4, 8, 2, mesh.shape["lev"]), ("ma_0", "ma_1", "ma_2", "lev"))
    return jax.shard_map(
        body,
        mesh=split,
        in_specs=(P("lev", None, MA, None), P(None, MA, None), P(), P()),
        out_specs=(P("lev", None, MA, None), P()),
        check_vma=False,
    )
```

profile of v0, /device:TPU:1, one launch (start us, length us, event | category | flops | bytes accessed | tf_op | source)
XLA Modules:
  0.0 245.4 jit_solution(4459062973413210070)
XLA Ops:
  7.2 0.0 all-gather.2.cloned.1.call-start
  7.3 0.1 fusion.23
  7.3 0.6 copy-done
  7.9 1.7 gather_fusion
  9.6 0.1 dynamic_slice.6
  9.7 0.8 add_divide_fusion
  10.5 3.3 %fusion.19 = f32[18,2,20,1280]{3,0,2,1:T(8,128)S(1)} fusion(f32[18,2,20,1280]{3,1,2,0:T(2,128)} %param.4, f32[20,1280]{1,0:T(8,128)S(1)} %fusion.23, f32[18,1280]{1,0:T(8,128)S(1)} %add_divide_fusion), kind=kLoop, calls=%fused_computation.23 | loop fusion | flops 1843200 | bytes 7567360 | tf_op jit(solution)/shard_map/mul | solution.py:86
  13.8 2.2 copy-done.1
  16.0 4.7 %copy.15 = f32[18,2,20,1280]{3,1,2,0:T(2,128)} copy(f32[18,2,20,1280]{3,0,2,1:T(8,128)S(1)} %fusion.19) | data formatting | bytes 7372800 | tf_op jit(solution)/shard_map/mul | solution.py:86
  20.7 0.0 all-gather.2.cloned.1.call-update
  20.7 5.2 %collective-permute-start.3 = (f32[18,2,20,1280]{3,1,2,0:T(2,128)}, f32[18,2,20,1280]{3,1,2,0:T(2,128)}, u32[]{:S(2)}, u32[]{:S(2)}) collective-permute-start(f32[18,2,20,1280]{3,1,2,0:T(2,128)} %copy.15), channel_id=1, source_target_pairs={{4,0},{8,4},{12,8},{16,12},{20,16},{24,20},{28,24},{32,28},{36,32}... | collective-permute-start | bytes 11059208 | tf_op jit(solution)/shard_map/ppermute | solution.py:17
  25.8 1.9 collective-permute-start.2
  27.8 1.3 collective-permute-start.1
  29.1 5.9 %collective-permute-start = (f32[18,2,20,1280]{3,1,2,0:T(2,128)}, f32[18,2,20,1280]{3,1,2,0:T(2,128)}, u32[]{:S(2)}, u32[]{:S(2)}) collective-permute-start(f32[18,2,20,1280]{3,1,2,0:T(2,128)} %copy.15), channel_id=1, source_target_pairs={{0,8},{4,12},{8,16},{12,20},{16,24},{20,28},{24,32},{28,36},{32,40... | collective-permute-start | bytes 11059208 | tf_op jit(solution)/shard_map/ppermute | solution.py:17
  35.1 0.3 fusion.44
  35.5 9.8 %fusion.41 = (f32[18,2,19,1280]{3,0,2,1:T(8,128)}, f32[18,2,19,1280]{3,0,2,1:T(8,128)}) fusion(f32[18,2,20,1280]{3,0,2,1:T(8,128)} %copy-done.1), kind=kLoop, calls=%fused_computation.75 | loop fusion | bytes 14008320 | tf_op jit(solution)/shard_map/slice | solution.py:35
  45.2 53.9 %collective-permute-done.2 = f32[18,2,20,1280]{3,1,2,0:T(2,128)} collective-permute-done((f32[18,2,20,1280]{3,1,2,0:T(2,128)}, f32[18,2,20,1280]{3,1,2,0:T(2,128)}, u32[]{:S(2)}, u32[]{:S(2)}) %collective-permute-start.2) | collective-permute-done | bytes 3686432 | tf_op jit(solution)/shard_map/ppermute | solution.py:17
  99.1 5.6 %fusion.42 = (f32[18,2,19,1280]{3,1,2,0:T(2,128)S(1)}, f32[18,2,19,1280]{3,1,2,0:T(2,128)S(1)}) fusion(f32[18,2,20,1280]{3,1,2,0:T(2,128)} %collective-permute-done.2), kind=kLoop, calls=%fused_computation.76 | loop fusion | bytes 14008320 | tf_op jit(solution)/shard_map/slice | solution.py:35
  104.6 2.5 %copy.141 = f32[18,2,19,1280]{3,0,2,1:T(8,128)} copy(f32[18,2,19,1280]{3,1,2,0:T(2,128)S(1)} %get-tuple-element.37) | data formatting | bytes 7004160
  107.1 2.6 %copy.139 = f32[18,2,19,1280]{3,0,2,1:T(8,128)} copy(f32[18,2,19,1280]{3,1,2,0:T(2,128)S(1)} %get-tuple-element.38) | data formatting | bytes 7004160
  109.8 5.5 %fusion.43 = (f32[18,2,19,1280]{3,1,2,0:T(2,128)S(1)}, f32[18,2,19,1280]{3,1,2,0:T(2,128)S(1)}) fusion(f32[18,2,20,1280]{3,1,2,0:T(2,128)} %collective-permute-done.3), kind=kLoop, calls=%fused_computation.77 | loop fusion | bytes 14008320 | tf_op jit(solution)/shard_map/slice | solution.py:35
  115.2 2.5 %copy.140 = f32[18,2,19,1280]{3,0,2,1:T(8,128)} copy(f32[18,2,19,1280]{3,1,2,0:T(2,128)S(1)} %get-tuple-element.39) | data formatting | bytes 7004160
  117.7 2.5 %copy.138 = f32[18,2,19,1280]{3,0,2,1:T(8,128)} copy(f32[18,2,19,1280]{3,1,2,0:T(2,128)S(1)} %get-tuple-element.40) | data formatting | bytes 7004160
  120.2 26.9 %collective-permute-done = f32[18,2,20,1280]{3,1,2,0:T(2,128)} collective-permute-done((f32[18,2,20,1280]{3,1,2,0:T(2,128)}, f32[18,2,20,1280]{3,1,2,0:T(2,128)}, u32[]{:S(2)}, u32[]{:S(2)}) %collective-permute-start) | collective-permute-done | bytes 3686432 | tf_op jit(solution)/shard_map/ppermute | solution.py:17
  147.1 17.0 %all-gather.2.cloned.1.call-done = f32[72,2,20,1280]{3,1,2,0:T(2,128)} async-done(((f32[18,2,20,1280]{3,1,2,0:T(2,128)}), f32[72,2,20,1280]{3,1,2,0:T(2,128)}) %all-gather.2.cloned.1.call-update) | async-done | bytes 14745616 | tf_op jit(solution)/shard_map/all_gather | solution.py:90
  164.1 27.1 %multiply_reduce_fusion = (f32[]{:T(128)}, f32[18,2,20,1280]{3,0,2,1:T(8,128)S(1)}, f32[]{:T(128)}) fusion(f32[20,1280]{1,0:T(8,128)S(1)} %fusion.23, f32[18,2,20,1280]{3,1,2,0:T(2,128)} %param.4, f32[18,1280]{1,0:T(8,128)S(1)} %add_divide_fusion, f32[20]{0:T(128)S(1)} %get-tuple-element.52, f32[20]{0:T(128)S(1)} %get-tuple-element.51, ...), kind=kOutput, calls=%fused_computation.25 | convolution fusion | flops 844185600 | bytes 58642956 | tf_op jit(solution)/shard_map/kl,lcin->kcin/dot_general | solution.py:87
  191.2 4.7 %copy.37 = f32[18,2,20,1280]{3,1,2,0:T(2,128)} copy(f32[18,2,20,1280]{3,0,2,1:T(8,128)S(1)} %get-tuple-element.33) | data formatting | bytes 7372800
  195.9 9.0 %all-reduce.8 = (f32[]{:T(128)}, f32[]{:T(128)}) all-reduce(f32[]{:T(128)} %get-tuple-element.32, f32[]{:T(128)} %get-tuple-element.36), channel_id=1, replica_groups=mesh['ma_0'=4,'ma_1'=8,'ma_2'=2,'lev'=4] {'ma_0'}, use_global_device_ids=true, to_apply=%region_6.7 | all-reduce | flops 2 | bytes 16 | tf_op jit(solution)/shard_map/psum | solution.py:22
  204.9 14.4 %all-reduce.6 = (f32[]{:T(128)}, f32[]{:T(128)}) all-reduce(f32[]{:T(128)} %get-tuple-element.12, f32[]{:T(128)} %get-tuple-element.13), channel_id=1, replica_groups=mesh['ma_0'=4,'ma_1'=8,'ma_2'=2,'lev'=4] {'ma_1'}, use_global_device_ids=true, to_apply=%region_7.8 | all-reduce | flops 2 | bytes 16 | tf_op jit(solution)/shard_map/psum | solution.py:22
  219.3 9.2 %all-reduce.9 = (f32[]{:T(128)}, f32[]{:T(128)}) all-reduce(f32[]{:T(128)} %get-tuple-element.8, f32[]{:T(128)} %get-tuple-element.9), channel_id=1, replica_groups=mesh['ma_0'=4,'ma_1'=8,'ma_2'=2,'lev'=4] {'ma_2'}, use_global_device_ids=true, to_apply=%region_8.9 | all-reduce | flops 2 | bytes 16 | tf_op jit(solution)/shard_map/psum | solution.py:22
  228.5 8.1 %all-reduce.7 = (f32[1]{0:T(128)}, f32[1]{0:T(128)}) all-reduce(f32[1]{0:T(128)} %bitcast.8, f32[1]{0:T(128)} %bitcast.7), channel_id=1, replica_groups=mesh['ma_0'=4,'ma_1'=8,'ma_2'=2,'lev'=4] {'lev'}, use_global_device_ids=true, to_apply=%region_9.10 | all-reduce | flops 2 | bytes 16 | tf_op jit(solution)/shard_map/psum | solution.py:22
  236.7 1.8 fusion.31
  (23 shorter events, 0.2 us)
Async XLA Ops:
  7.2 0.8 copy-start
  7.2 156.9 %all-gather.2.cloned.1.call-start = ((), (), s32[]{:S(2)}) async-start(), calls=%async_computation | async-start | bytes 18432000 | tf_op jit(solution)/shard_map/all_gather | solution.py:90
  13.8 2.2 copy-start.1
  16.0 19.1 %copy-start.2 = (f32[4,20,1280]{2,0,1:T(4,128)S(1)}, f32[4,20,1280]{2,0,1:T(4,128)}, u32[]{:S(2)}) copy-start(f32[4,20,1280]{2,0,1:T(4,128)} %param.5) | copy-start | bytes 1228804
  20.7 89.1 %collective-permute-start.3 = (f32[18,2,20,1280]{3,1,2,0:T(2,128)}, f32[18,2,20,1280]{3,1,2,0:T(2,128)}, u32[]{:S(2)}, u32[]{:S(2)}) collective-permute-start(f32[18,2,20,1280]{3,1,2,0:T(2,128)} %copy.15), channel_id=1, source_target_pairs={{4,0},{8,4},{12,8},{16,12},{20,16},{24,20},{28,24},{32,28},{36,32}... | collective-permute-start | bytes 11059208 | tf_op jit(solution)/shard_map/ppermute | solution.py:17
  25.8 73.2 %collective-permute-start.2 = (f32[18,2,20,1280]{3,1,2,0:T(2,128)}, f32[18,2,20,1280]{3,1,2,0:T(2,128)}, u32[]{:S(2)}, u32[]{:S(2)}) collective-permute-start(f32[18,2,20,1280]{3,1,2,0:T(2,128)} %copy.15), channel_id=1, source_target_pairs={{0,4},{4,8},{8,12},{12,16},{16,20},{20,24},{24,28},{28,32},{32,36}... | collective-permute-start | bytes 11059208 | tf_op jit(solution)/shard_map/ppermute | solution.py:17
  27.8 92.4 %collective-permute-start.1 = (f32[18,2,20,1280]{3,1,2,0:T(2,128)}, f32[18,2,20,1280]{3,1,2,0:T(2,128)}, u32[]{:S(2)}, u32[]{:S(2)}) collective-permute-start(f32[18,2,20,1280]{3,1,2,0:T(2,128)} %copy.15), channel_id=1, source_target_pairs={{8,0},{12,4},{16,8},{20,12},{24,16},{28,20},{32,24},{36,28},{40,32... | collective-permute-start | bytes 11059208 | tf_op jit(solution)/shard_map/ppermute | solution.py:17
  29.1 118.0 %collective-permute-start = (f32[18,2,20,1280]{3,1,2,0:T(2,128)}, f32[18,2,20,1280]{3,1,2,0:T(2,128)}, u32[]{:S(2)}, u32[]{:S(2)}) collective-permute-start(f32[18,2,20,1280]{3,1,2,0:T(2,128)} %copy.15), channel_id=1, source_target_pairs={{0,8},{4,12},{8,16},{12,20},{16,24},{20,28},{24,32},{28,36},{32,40... | collective-permute-start | bytes 11059208 | tf_op jit(solution)/shard_map/ppermute | solution.py:17
  117.7 46.4 %copy-start.3 = (f32[1280]{0:T(1024)S(1)}, f32[1280]{0:T(1024)}, u32[]{:S(2)}) copy-start(f32[1280]{0:T(1024)} %param.6) | copy-start | bytes 15364
Sparse Core Ops, SparseCore 0:
  20.8 143.2 all-gather.1
where the time goes:
time: 246 us; the launch traced here: 245 us
  waiting for transfers between devices  97.8 us (40%)
  local copies, waits for them, and re-layouts  45.2 us (18%)
  blocking collectives  40.8 us (17%)
  matrix products  27.1 us (11%)
  starting transfers between devices  14.3 us (6%)
  between operations  14.2 us (6%)
  other arithmetic  6.09 us (2%)
    ppermute x4, waiting for transfers between devices, shifted(): return lax.ppermute(block, axis, route)  80.7 us
    psum x4, blocking collectives, by_axis(): x = lax.psum(x, axis)  40.8 us
    dot_general x1, matrix products, body(): jnp.einsum('kl,lcin->kcin', weights, lax.all_gather(first, 'lev', axis=0,...  27.1 us
    slice x3, local copies, waits for them, and re-layouts, next_row(): return jnp.concatenate([empty, block[:, :, :-1]], axis=2)  20.8 us
    unnamed x13, local copies, waits for them, and re-layouts  17.6 us
    all_gather x1, waiting for transfers between devices, body(): lax.all_gather(first, 'lev', axis=0, tiled=True)  17 us
    ppermute x4, starting transfers between devices, shifted(): return lax.ppermute(block, axis, route)  14.2 us
  transfers between devices with their start and end apart: 5, of which 3 were waited for; matrix products, arithmetic and copies ran while one was open for 13% of the time, Pallas kernels for 0%

commit v1 on v0

--- a/solution.py
+++ b/solution.py
@@ -87,7 +87,9 @@
     mixed = jnp.einsum(
         "kl,lcin->kcin",
         weights,
-        lax.all_gather(first, "lev", axis=0, tiled=True),
+        jnp.concatenate(
+            lax.all_to_all(jnp.stack([first] * lax.axis_size("lev")), "lev", 0, 0), axis=0
+        ),
         precision=lax.Precision.HIGHEST,
     )
     nearby = square_neighbours(first)

time: 246 us -> 267 us (1.085)
  waiting for transfers between devices: 97.8 us -> 117 us
  between operations: 14.2 us -> 0.85 us
  starting transfers between devices: 14.3 us -> 20.5 us
  blocking collectives: 40.8 us -> 45.3 us
  local copies, waits for them, and re-layouts: 45.2 us -> 48.9 us
    all_to_all x0 -> x1, waiting for transfers between devices: none -> 34.1 us  [body(): lax.all_to_all(jnp.stack([first] * lax.axis_size('lev')), 'lev', 0, 0)]
    all_gather x1 -> x0, waiting for transfers between devices: 17 us -> none  [body(): lax.all_gather(first, 'lev', axis=0, tiled=True)]
    all_to_all x0 -> x1, starting transfers between devices: none -> 6.79 us  [body(): lax.all_to_all(jnp.stack([first] * lax.axis_size('lev')), 'lev', 0, 0)]
    another operation x0 -> x1, local copies, waits for them, and re-layouts: none -> 5.7 us  [body(): jnp.stack([first] * lax.axis_size('lev'))]
    psum x4, blocking collectives: 40.8 us -> 45.3 us  [by_axis(): x = lax.psum(x, axis)]
    unnamed x13 -> x15, local copies, waits for them, and re-layouts: 17.6 us -> 19.3 us
  transfers between devices with their start and end apart: 5 -> 5, of which waited for: 3 -> 3; matrix products, arithmetic and copies ran while one was open for 13% -> 11% of each run, Pallas kernels for 0% -> 0%
where the time goes in v1:
time: 267 us; the launch traced here: 266 us
  waiting for transfers between devices  117 us (44%)
  local copies, waits for them, and re-layouts  48.9 us (18%)
  blocking collectives  45.3 us (17%)
  matrix products  27.2 us (10%)
  starting transfers between devices  20.5 us (8%)
  other arithmetic  6.09 us (2%)
    ppermute x4, waiting for transfers between devices, shifted(): return lax.ppermute(block, axis, route)  83.2 us
    psum x4, blocking collectives, by_axis(): x = lax.psum(x, axis)  45.3 us
    all_to_all x1, waiting for transfers between devices, body(): lax.all_to_all(jnp.stack([first] * lax.axis_size('lev')), 'lev', 0, 0)  34.1 us
    dot_general x1, matrix products, body(): jnp.einsum('kl,lcin->kcin', weights, jnp.concatenate(lax.all_to_all(jnp.s...  27.2 us
    unnamed x15, local copies, waits for them, and re-layouts  19.3 us
    slice x3, local copies, waits for them, and re-layouts, next_row(): return jnp.concatenate([empty, block[:, :, :-1]], axis=2)  18.9 us
    ppermute x4, starting transfers between devices, shifted(): return lax.ppermute(block, axis, route)  13.7 us
    all_to_all x1, starting transfers between devices, body(): lax.all_to_all(jnp.stack([first] * lax.axis_size('lev')), 'lev', 0, 0)  6.79 us
  transfers between devices with their start and end apart: 5, of which 3 were waited for; matrix products, arithmetic and copies ran while one was open for 11% of the time, Pallas kernels for 0%

profile of v1, /device:TPU:1, one launch (start us, length us, event | category | flops | bytes accessed | tf_op | source)
XLA Modules:
  0.0 266.1 jit_solution(14628822558401353184)
XLA Ops:
  0.8 0.6 copy-done
  1.4 1.7 gather_fusion
  3.1 0.1 dynamic_slice.6
  3.2 0.8 add_divide_fusion
  4.0 3.3 %fusion.19 = f32[18,2,20,1280]{3,0,2,1:T(8,128)S(1)} fusion(f32[18,2,20,1280]{3,1,2,0:T(2,128)} %param.4, f32[20,1280]{1,0:T(8,128)S(1)} %fusion.23, f32[18,1280]{1,0:T(8,128)S(1)} %add_divide_fusion), kind=kLoop, calls=%fused_computation.23 | loop fusion | flops 1843200 | bytes 7567360 | tf_op jit(solution)/shard_map/mul | solution.py:86
  7.2 2.2 copy-done.1
  9.4 2.8 %copy.17 = f32[18,2,20,1280]{3,1,2,0:T(2,128)S(1)} copy(f32[18,2,20,1280]{3,0,2,1:T(8,128)S(1)} %fusion.19) | data formatting | bytes 7372800 | tf_op jit(solution)/shard_map/mul | solution.py:86
  12.3 1.8 copy-done.2
  14.1 5.7 %stack.16 = f32[4,18,2,20,1280]{4,2,3,1,0:T(2,128)} broadcast(f32[18,2,20,1280]{3,1,2,0:T(2,128)S(1)} %copy.17), dimensions={1,2,3,4} | broadcast | bytes 18432000 | tf_op jit(solution)/shard_map/stack | solution.py:91
  19.8 6.8 %all-to-all-start = ((f32[4,18,2,20,1280]{4,2,3,1,0:T(2,128)}), f32[4,18,2,20,1280]{4,2,3,1,0:T(2,128)}, u32[]{:S(2)}, u32[]{:S(2)}) async-start(f32[4,18,2,20,1280]{4,2,3,1,0:T(2,128)} %stack.16), calls=%async_computation | async-start | bytes 29491200 | tf_op jit(solution)/shard_map/all_to_all | solution.py:91
  26.6 5.2 %collective-permute-start.3 = (f32[18,2,20,1280]{3,1,2,0:T(2,128)}, f32[18,2,20,1280]{3,1,2,0:T(2,128)}, u32[]{:S(2)}, u32[]{:S(2)}) collective-permute-start(f32[18,2,20,1280]{3,1,2,0:T(2,128)} %copy-done.2), channel_id=1, source_target_pairs={{4,0},{8,4},{12,8},{16,12},{20,16},{24,20},{28,24},{32,28},{36,32}... | collective-permute-start | bytes 11059208 | tf_op jit(solution)/shard_map/ppermute | solution.py:17
  31.8 1.9 collective-permute-start.2
  33.7 5.2 %collective-permute-start = (f32[18,2,20,1280]{3,1,2,0:T(2,128)}, f32[18,2,20,1280]{3,1,2,0:T(2,128)}, u32[]{:S(2)}, u32[]{:S(2)}) collective-permute-start(f32[18,2,20,1280]{3,1,2,0:T(2,128)} %copy-done.2), channel_id=1, source_target_pairs={{0,8},{4,12},{8,16},{12,20},{16,24},{20,28},{24,32},{28,36},{32,40... | collective-permute-start | bytes 11059208 | tf_op jit(solution)/shard_map/ppermute | solution.py:17
  38.9 1.5 collective-permute-start.1
  40.5 0.3 fusion.44
  40.9 7.9 %fusion.41 = (f32[18,2,19,1280]{3,0,2,1:T(8,128)}, f32[18,2,19,1280]{3,0,2,1:T(8,128)}) fusion(f32[18,2,20,1280]{3,0,2,1:T(8,128)} %copy-done.1), kind=kLoop, calls=%fused_computation.75 | loop fusion | bytes 14008320 | tf_op jit(solution)/shard_map/slice | solution.py:35
  48.8 53.1 %collective-permute-done.3 = f32[18,2,20,1280]{3,1,2,0:T(2,128)} collective-permute-done((f32[18,2,20,1280]{3,1,2,0:T(2,128)}, f32[18,2,20,1280]{3,1,2,0:T(2,128)}, u32[]{:S(2)}, u32[]{:S(2)}) %collective-permute-start.3) | collective-permute-done | bytes 3686432 | tf_op jit(solution)/shard_map/ppermute | solution.py:17
  101.9 5.5 %fusion.43 = (f32[18,2,19,1280]{3,1,2,0:T(2,128)S(1)}, f32[18,2,19,1280]{3,1,2,0:T(2,128)S(1)}) fusion(f32[18,2,20,1280]{3,1,2,0:T(2,128)} %collective-permute-done.3), kind=kLoop, calls=%fused_computation.77 | loop fusion | bytes 14008320 | tf_op jit(solution)/shard_map/slice | solution.py:35
  107.4 2.5 copy.140
  109.8 5.6 %fusion.42 = (f32[18,2,19,1280]{3,1,2,0:T(2,128)S(1)}, f32[18,2,19,1280]{3,1,2,0:T(2,128)S(1)}) fusion(f32[18,2,20,1280]{3,1,2,0:T(2,128)} %collective-permute-done.2), kind=kLoop, calls=%fused_computation.76 | loop fusion | bytes 14008320 | tf_op jit(solution)/shard_map/slice | solution.py:35
  115.4 2.5 copy.141
  117.9 2.5 copy.142
  120.4 2.5 copy.143
  122.9 30.0 %collective-permute-done = f32[18,2,20,1280]{3,1,2,0:T(2,128)} collective-permute-done((f32[18,2,20,1280]{3,1,2,0:T(2,128)}, f32[18,2,20,1280]{3,1,2,0:T(2,128)}, u32[]{:S(2)}, u32[]{:S(2)}) %collective-permute-start) | collective-permute-done | bytes 3686432 | tf_op jit(solution)/shard_map/ppermute | solution.py:17
  153.0 34.1 %all-to-all-done = f32[4,18,2,20,1280]{4,2,3,1,0:T(2,128)} async-done(((f32[4,18,2,20,1280]{4,2,3,1,0:T(2,128)}), f32[4,18,2,20,1280]{4,2,3,1,0:T(2,128)}, u32[]{:S(2)}, u32[]{:S(2)}) %all-to-all-start) | async-done | bytes 14745632 | tf_op jit(solution)/shard_map/all_to_all | solution.py:91
  187.1 27.2 %multiply_reduce_fusion = (f32[]{:T(128)}, f32[18,2,20,1280]{3,0,2,1:T(8,128)S(1)}, f32[]{:T(128)}) fusion(f32[20,1280]{1,0:T(8,128)S(1)} %fusion.23, f32[18,2,20,1280]{3,1,2,0:T(2,128)} %param.4, f32[18,1280]{1,0:T(8,128)S(1)} %add_divide_fusion, f32[20]{0:T(128)S(1)} %get-tuple-element.52, f32[20]{0:T(128)S(1)} %get-tuple-element.51, ...), kind=kOutput, calls=%fused_computation.25 | convolution fusion | flops 844185600 | bytes 58642956 | tf_op jit(solution)/shard_map/kl,lcin->kcin/dot_general | solution.py:87
  214.3 4.7 %copy.39 = f32[18,2,20,1280]{3,1,2,0:T(2,128)} copy(f32[18,2,20,1280]{3,0,2,1:T(8,128)S(1)} %get-tuple-element.33) | data formatting | bytes 7372800
  218.9 10.9 %all-reduce.8 = (f32[]{:T(128)}, f32[]{:T(128)}) all-reduce(f32[]{:T(128)} %get-tuple-element.32, f32[]{:T(128)} %get-tuple-element.36), channel_id=1, replica_groups=mesh['ma_0'=4,'ma_1'=8,'ma_2'=2,'lev'=4] {'ma_0'}, use_global_device_ids=true, to_apply=%region_6.7 | all-reduce | flops 2 | bytes 16 | tf_op jit(solution)/shard_map/psum | solution.py:22
  229.9 16.9 %all-reduce.6 = (f32[]{:T(128)}, f32[]{:T(128)}) all-reduce(f32[]{:T(128)} %get-tuple-element.12, f32[]{:T(128)} %get-tuple-element.13), channel_id=1, replica_groups=mesh['ma_0'=4,'ma_1'=8,'ma_2'=2,'lev'=4] {'ma_1'}, use_global_device_ids=true, to_apply=%region_7.8 | all-reduce | flops 2 | bytes 16 | tf_op jit(solution)/shard_map/psum | solution.py:22
  246.8 10.0 %all-reduce.9 = (f32[]{:T(128)}, f32[]{:T(128)}) all-reduce(f32[]{:T(128)} %get-tuple-element.8, f32[]{:T(128)} %get-tuple-element.9), channel_id=1, replica_groups=mesh['ma_0'=4,'ma_1'=8,'ma_2'=2,'lev'=4] {'ma_2'}, use_global_device_ids=true, to_apply=%region_8.9 | all-reduce | flops 2 | bytes 16 | tf_op jit(solution)/shard_map/psum | solution.py:22
  256.8 7.5 %all-reduce.7 = (f32[1]{0:T(128)}, f32[1]{0:T(128)}) all-reduce(f32[1]{0:T(128)} %bitcast.9, f32[1]{0:T(128)} %bitcast.8), channel_id=1, replica_groups=mesh['ma_0'=4,'ma_1'=8,'ma_2'=2,'lev'=4] {'lev'}, use_global_device_ids=true, to_apply=%region_9.10 | all-reduce | flops 2 | bytes 16 | tf_op jit(solution)/shard_map/psum | solution.py:22
  264.3 1.8 fusion.31
  (25 shorter events, 0.3 us)
Async XLA Ops:
  0.6 0.8 copy-start
  7.2 2.2 copy-start.1
  12.3 1.8 copy-start.2
  19.8 20.7 %copy-start.3 = (f32[4,20,1280]{2,0,1:T(4,128)S(1)}, f32[4,20,1280]{2,0,1:T(4,128)}, u32[]{:S(2)}) copy-start(f32[4,20,1280]{2,0,1:T(4,128)} %param.5) | copy-start | bytes 1228804
  19.8 167.3 %all-to-all-start = ((f32[4,18,2,20,1280]{4,2,3,1,0:T(2,128)}), f32[4,18,2,20,1280]{4,2,3,1,0:T(2,128)}, u32[]{:S(2)}, u32[]{:S(2)}) async-start(f32[4,18,2,20,1280]{4,2,3,1,0:T(2,128)} %stack.16), calls=%async_computation | async-start | bytes 29491200 | tf_op jit(solution)/shard_map/all_to_all | solution.py:91
  26.6 75.3 %collective-permute-start.3 = (f32[18,2,20,1280]{3,1,2,0:T(2,128)}, f32[18,2,20,1280]{3,1,2,0:T(2,128)}, u32[]{:S(2)}, u32[]{:S(2)}) collective-permute-start(f32[18,2,20,1280]{3,1,2,0:T(2,128)} %copy-done.2), channel_id=1, source_target_pairs={{4,0},{8,4},{12,8},{16,12},{20,16},{24,20},{28,24},{32,28},{36,32}... | collective-permute-start | bytes 11059208 | tf_op jit(solution)/shard_map/ppermute | solution.py:17
  31.8 78.1 %collective-permute-start.2 = (f32[18,2,20,1280]{3,1,2,0:T(2,128)}, f32[18,2,20,1280]{3,1,2,0:T(2,128)}, u32[]{:S(2)}, u32[]{:S(2)}) collective-permute-start(f32[18,2,20,1280]{3,1,2,0:T(2,128)} %copy-done.2), channel_id=1, source_target_pairs={{0,4},{4,8},{8,12},{12,16},{16,20},{20,24},{24,28},{28,32},{32,36}... | collective-permute-start | bytes 11059208 | tf_op jit(solution)/shard_map/ppermute | solution.py:17
  33.7 119.3 %collective-permute-start = (f32[18,2,20,1280]{3,1,2,0:T(2,128)}, f32[18,2,20,1280]{3,1,2,0:T(2,128)}, u32[]{:S(2)}, u32[]{:S(2)}) collective-permute-start(f32[18,2,20,1280]{3,1,2,0:T(2,128)} %copy-done.2), channel_id=1, source_target_pairs={{0,8},{4,12},{8,16},{12,20},{16,24},{20,28},{24,32},{28,36},{32,40... | collective-permute-start | bytes 11059208 | tf_op jit(solution)/shard_map/ppermute | solution.py:17
  38.9 114.1 %collective-permute-start.1 = (f32[18,2,20,1280]{3,1,2,0:T(2,128)}, f32[18,2,20,1280]{3,1,2,0:T(2,128)}, u32[]{:S(2)}, u32[]{:S(2)}) collective-permute-start(f32[18,2,20,1280]{3,1,2,0:T(2,128)} %copy-done.2), channel_id=1, source_target_pairs={{8,0},{12,4},{16,8},{20,12},{24,16},{28,20},{32,24},{36,28},{40,32... | collective-permute-start | bytes 11059208 | tf_op jit(solution)/shard_map/ppermute | solution.py:17
  120.4 66.7 %copy-start.4 = (f32[1280]{0:T(1024)S(1)}, f32[1280]{0:T(1024)}, u32[]{:S(2)}) copy-start(f32[1280]{0:T(1024)} %param.6) | copy-start | bytes 15364
